TPU v7x, 32 devices: a whole 2x2x4 slice. The times are simulated.
32 devices in a mesh: row: 8 (over y, x, core), col: 4 (over z).
Axes of the slice: x: 2, y: 2, z: 4, core: 2. Of those that a mesh axis runs over, the one named last changes fastest.
Arguments:
- legendre: bfloat16 [4, 128, 89, 8, 128], P(None, 'col', None, 'row'), may hold values from -6 to 6
- longitude: float32 [512], replicated, may hold values from -3.140625 to 3.140625
- obs_weight: float32 [512], replicated, may hold values from 0.1 to 1.9
- span_weight: float32 [8], replicated, may hold values from 0.3 to 3
- span_of: int32 [512], replicated, may hold values from 0 to 7
- tile_order: int32 [712], replicated, may hold values from 0 to 711, each once
- slab_start: int32 [1], replicated, may hold values from 0 to 704
- resident: float32 [89, 8, 4, 128, 128], P(None, 'row', 'col'), may hold values from -6 to 6
Outputs:
- updated: float32 [89, 8, 4, 128, 128], P(None, 'row', 'col')
Inputs may be any that keep to these rules, and one draw needn't show every extreme that they name: tile_order is a permutation of the slot positions.
All inputs are finite; a program needn't handle non-finite values.
Results may differ from a plain program's by a relative error of at most 0.00074.
Values may be sent and summed in bfloat16 or wider, within the bound.
No kernel may reach another device: no remote copies, remote signals or barrier semaphores. Data moves between devices by JAX's collectives and lax.ppermute only.
A program may use at most 64 MiB of HBM per device.

v0:
```python
import math
import jax
import jax.numpy as jnp
from jax import lax
from jax.sharding import PartitionSpec as P

DEGREE = 300
UNK = 90600


def lookup_weights(obs_weight, span_weight, span_of):
    group_count = span_weight.shape[0]
    matches = span_of[:, None] == jnp.arange(group_count, dtype=jnp.int32)[None, :]
    factor = jnp.sum(jnp.where(matches, span_weight[None, :], 0.0), axis=1)
    return obs_weight * factor * (0.25 / math.sqrt(obs_weight.shape[0]))


def locate(tile_order, targets):
    places = jnp.arange(tile_order.shape[0], dtype=jnp.int32)
    return jnp.sum(jnp.where(tile_order[None, :] == targets[:, None], places[None, :], 0), axis=1)


def contract_rows(left_side, right_side):
    return lax.dot_general(
        left_side, right_side, (((0,), (0,)), ((), ())), preferred_element_type=jnp.float32
    )


def per_device(
    legendre, longitude, obs_weight, span_weight, span_of, tile_order, slab_start, resident
):
    block_count, shard_rows, slot_count, _, tile_size = legendre.shape
    row_count = lax.axis_size("row")
    col_count = lax.axis_size("col")
    row_index = lax.axis_index("row")
    col_index = lax.axis_index("col")
    block_rows = shard_rows * col_count
    order_map = tile_order.reshape(slot_count, row_count)
    own_tiles = lax.dynamic_slice_in_dim(order_map, row_index, 1, 1)[:, 0]
    unknown = own_tiles[:, None] * tile_size + jnp.arange(tile_size, dtype=jnp.int32)[None, :]
    orders = (unknown % (DEGREE + 1)).astype(jnp.float32).reshape(1, slot_count * tile_size)
    is_valid = (unknown < UNK).reshape(1, slot_count * tile_size)
    targets = slab_start[0] + jnp.arange(col_count, dtype=jnp.int32)
    positions = locate(tile_order, targets)
    target = targets[col_index]
    root_row = positions[col_index] % row_count
    root_slots = positions // row_count
    root_slot = root_slots[col_index]
    is_root = row_index == root_row
    weights = lookup_weights(obs_weight, span_weight, span_of).reshape(block_count, block_rows)
    angles = longitude.reshape(block_count, block_rows)
    in_lower = own_tiles >= target
    zero_piece = jnp.zeros((), jnp.bfloat16)
    all_values = legendre.reshape(block_count * shard_rows, slot_count * tile_size)
    own_angles = lax.dynamic_slice_in_dim(angles, col_index * shard_rows, shard_rows, 1)
    own_angles = own_angles.reshape(block_count * shard_rows)
    design_all = jnp.where(
        is_valid, all_values.astype(jnp.float32) * jnp.cos(own_angles[:, None] * orders), 0.0
    ).astype(jnp.bfloat16)
    design_all = design_all.reshape(block_count, shard_rows, slot_count * tile_size)
    gathered = lax.all_gather(design_all, "col", axis=1, tiled=True)
    gathered = gathered.reshape(block_count * block_rows, slot_count * tile_size)
    candidate = lax.dynamic_slice_in_dim(gathered, root_slot * tile_size, tile_size, 1)
    column = lax.psum(jnp.where(is_root, candidate, zero_piece), "row").astype(jnp.float32)
    weighted = (weights.reshape(block_count * block_rows)[:, None] * column).astype(jnp.bfloat16)
    running = contract_rows(gathered, weighted)
    update = jnp.where(
        in_lower[:, None, None], running.reshape(slot_count, tile_size, tile_size), 0.0
    )
    return resident + update.reshape(resident.shape)


def solution(mesh):
    placed = (
        P(None, "col", None, "row", None),
        P(),
        P(),
        P(),
        P(),
        P(),
        P(),
        P(None, "row", "col", None, None),
    )
    return jax.shard_map(
        per_device,
        mesh=mesh,
        in_specs=placed,
        out_specs=P(None, "row", "col", None, None),
        check_vma=False,
    )
```

profile of v0, /device:TPU:0, one launch (start us, length us, event | category | flops | bytes accessed | tf_op | source)
XLA Modules:
  0.0 322.1 jit_solution(3542823524447298766)
XLA Ops:
  6.5 0.0 copy-start
  6.5 0.0 all-gather.2.cloned.1.call-start
  6.5 0.8 reshape.90
  7.3 0.2 multiply_reduce_fusion
  7.5 0.1 fusion.4
  7.6 0.1 fusion.8
  7.7 5.5 %copy.20 = f32[4,32,89,1,128]{4,2,1,0,3:T(8,128)} copy(bf16[4,32,89,1,128]{4,1,3,2,0:T(8,128)(2,1)} %param.8) | data formatting | bytes 8749056 | tf_op jit(solution)/shard_map/convert_element_type | solution.py:58
  13.2 7.2 %reshape.94 = f32[4,32,11392]{2,1,0:T(8,128)} reshape(f32[4,32,89,1,128]{4,2,1,0,3:T(8,128)} %copy.20) | data formatting | bytes 11665408 | tf_op jit(solution)/shard_map/convert_element_type | solution.py:58
  20.4 0.0 copy-done
  20.4 0.1 constant_dynamic-slice_fusion
  20.5 0.0 copy-start.1
  20.5 0.0 copy-start.3
  20.5 0.0 copy-start.4
  20.5 22.0 %select_convert_fusion = bf16[4,32,11392]{2,1,0:T(8,128)(2,1)} fusion(f32[4,32,11392]{2,1,0:T(8,128)} %reshape.94, f32[11392]{0:T(1024)S(1)} %fusion.4, f32[4,32]{1,0:T(4,128)S(1)} %constant_dynamic-slice_fusion, pred[11392]{0:T(1024)(128)(4,1)S(1)} %fusion.8), kind=kLoop, calls=%fused_computation.2 | loop fusion | flops 5832704 | bytes 8806528 | tf_op jit(solution)/shard_map/convert_element_type | solution.py:59
  42.6 0.0 all-gather.2.cloned.1.call-update
  42.6 0.0 all-reduce.2.cloned.1.call-start
  43.3 0.0 copy-done.1
  43.3 0.2 select_reduce_fusion.1
  43.5 0.6 dynamic_slice.21
  46.0 0.6 dynamic_slice.22
  47.3 0.0 copy-done.3
  47.3 0.0 copy-done.4
  47.3 0.1 select_reduce_fusion
  47.4 201.2 %all-gather.2.cloned.1.call-done = bf16[4,128,11392]{2,1,0:T(8,128)(2,1)} async-done(((bf16[4,32,11392]{2,1,0:T(8,128)(2,1)}), bf16[4,128,11392]{2,1,0:T(8,128)(2,1)}) %all-gather.2.cloned.1.call-update) | async-done | bytes 11665424 | tf_op jit(solution)/shard_map/all_gather | solution.py:61
  248.6 1.6 dynamic-slice_select_fusion
  250.2 0.0 all-reduce.2.cloned.1.call-update
  250.3 0.0 copy-done.2
  250.3 0.6 dynamic_slice.19
  250.9 0.8 compare_reduce_fusion
  251.7 16.2 %copy.21 = bf16[11392,512]{1,0:T(8,128)(2,1)} copy(bf16[11392,512]{0,1:T(8,128)(2,1)} %bitcast.39) | data formatting | bytes 23330816 | tf_op jit(solution)/shard_map/dot_general | solution.py:24
  267.9 35.4 %all-reduce.2.cloned.1.call-done = bf16[512,128]{1,0:T(8,128)(2,1)} async-done(((bf16[512,128]{1,0:T(8,128)(2,1)}), bf16[512,128]{1,0:T(8,128)(2,1)}) %all-reduce.2.cloned.1.call-update) | async-done | bytes 131088 | tf_op jit(solution)/shard_map/psum | solution.py:64
  303.3 11.9 %fusion = f32[89,1,1,128,128]{4,3,2,1,0:T(8,128)} fusion(f32[89,1,1,128,128]{4,3,2,1,0:T(8,128)} %param.15, pred[89]{0:T(512)(128)(4,1)S(1)} %compare_reduce_fusion, bf16[89,128,512]{2,1,0:T(8,128)(2,1)} %bitcast.37, bf16[512,128]{1,0:T(8,128)(2,1)} %all-reduce.2.cloned.1.call-done, f32[512]{0:T(512)S(1)} %multiply_multiply_fusion), kind=kOutput, calls=%fused_computation.1 | convolution fusion | flops 1496285184 | bytes 23464024 | tf_op jit(solution)/shard_map/dot_general | solution.py:24
  (4 shorter events, 0.0 us)
Async XLA Ops:
  6.5 13.9 %copy-start = (f32[512]{0:T(512)S(1)}, f32[512]{0:T(512)}, u32[]{:S(2)}) copy-start(f32[512]{0:T(512)} %param.9) | copy-start | bytes 6148
  6.5 242.1 %all-gather.2.cloned.1.call-start = ((), (), s32[]{:S(2)}) async-start(), calls=%async_computation | async-start | bytes 14581760 | tf_op jit(solution)/shard_map/all_gather | solution.py:61
  20.5 22.8 %copy-start.1 = (s32[712]{0:T(1024)S(1)}, s32[712]{0:T(1024)}, u32[]{:S(2)}) copy-start(s32[712]{0:T(1024)} %param.13) | copy-start | bytes 8548
  20.5 26.8 %copy-start.3 = (s32[512]{0:T(512)S(1)}, s32[512]{0:T(512)}, u32[]{:S(2)}) copy-start(s32[512]{0:T(512)} %param.12) | copy-start | bytes 6148
  20.5 26.8 %copy-start.4 = (f32[8]{0:T(128)S(1)}, f32[8]{0:T(128)}, u32[]{:S(2)}) copy-start(f32[8]{0:T(128)} %param.11) | copy-start | bytes 100
  20.5 229.8 %copy-start.2 = (f32[512]{0:T(512)S(1)}, f32[512]{0:T(512)}, u32[]{:S(2)}) copy-start(f32[512]{0:T(512)} %param.10) | copy-start | bytes 6148
  42.6 260.7 %all-reduce.2.cloned.1.call-start = ((), (), s32[]{:S(2)}) async-start(), calls=%async_computation.1 | async-start | bytes 262144 | tf_op jit(solution)/shard_map/psum | solution.py:64
Sparse Core Ops, SparseCore 0:
  42.7 205.8 all-gather.1
  251.7 51.6 all-reduce.1
where the time goes:
time: 323 us; the launch traced here: 322 us
  waiting for transfers between devices  237 us (73%)
  local copies, waits for them, and re-layouts  31.5 us (10%)
  other arithmetic  25.1 us (8%)
  between operations  16.8 us (5%)
  matrix products  11.9 us (4%)
    all_gather x1, waiting for transfers between devices, per_device(): gathered = lax.all_gather(design_all, 'col', axis=1, tiled=True)  201 us
    psum x1, waiting for transfers between devices, per_device(): lax.psum(jnp.where(is_root, candidate, zero_piece), 'row')  35.4 us
    convert_element_type x1, other arithmetic, per_device(): design_all = jnp.where(is_valid, all_values.astype(jnp.float32) * jnp.cos...  22 us
    dot_general x1, local copies, waits for them, and re-layouts, contract_rows(): lax.dot_general(left_side, right_side, (((0,), (0,)), ((), ())), preferre...  16.2 us
    convert_element_type x2, local copies, waits for them, and re-layouts, per_device(): all_values.astype(jnp.float32) * jnp.cos(own_angles[:, None] * orders)  12.7 us
    dot_general x1, matrix products, contract_rows(): lax.dot_general(left_side, right_side, (((0,), (0,)), ((), ())), preferre...  11.9 us
  transfers between devices with their start and end apart: 2, of which 2 were waited for; matrix products, arithmetic and copies ran while one was open for 6% of the time, Pallas kernels for 0%

commit v1 on v0

--- a/solution.py
+++ b/solution.py
@@ -58,7 +58,12 @@
         is_valid, all_values.astype(jnp.float32) * jnp.cos(own_angles[:, None] * orders), 0.0
     ).astype(jnp.bfloat16)
     design_all = design_all.reshape(block_count, shard_rows, slot_count * tile_size)
-    gathered = lax.all_gather(design_all, "col", axis=1, tiled=True)
+    ring = [design_all]
+    for hop in range(3):
+        ring.append(lax.ppermute(ring[-1], "col", [(dev, (dev + 1) % 4) for dev in range(4)]))
+    gathered = jnp.roll(
+        jnp.concatenate(ring[::-1], axis=1), (lax.axis_index("col") + 1) * ring[0].shape[1], axis=1
+    )
     gathered = gathered.reshape(block_count * block_rows, slot_count * tile_size)
     candidate = lax.dynamic_slice_in_dim(gathered, root_slot * tile_size, tile_size, 1)
     column = lax.psum(jnp.where(is_root, candidate, zero_piece), "row").astype(jnp.float32)

time: 323 us -> 368 us (1.14)
  other arithmetic: 25.1 us -> 62.4 us
  local copies, waits for them, and re-layouts: 31.5 us -> 46.6 us
  waiting for transfers between devices: 237 us -> 226 us
    all_gather x1 -> x0, waiting for transfers between devices: 201 us -> none  [per_device(): gathered = lax.all_gather(design_all, 'col', axis=1, tiled=True)]
    ppermute x0 -> x3, waiting for transfers between devices: none -> 193 us  [per_device(): lax.ppermute(ring[-1], 'col', [(dev, (dev + 1) % 4) for dev in range(4)])]
    unnamed x0 -> x2, other arithmetic: none -> 19.6 us
    concatenate x0 -> x1, other arithmetic: none -> 19.4 us  [per_device(): jnp.roll(jnp.concatenate(ring[::-1], axis=1), (lax.axis_index('col') + 1)...]
    unnamed x10 -> x24, local copies, waits for them, and re-layouts: 0.02 us -> 14.2 us
  transfers between devices with their start and end apart: 2 -> 4, of which waited for: 2 -> 4; matrix products, arithmetic and copies ran while one was open for 6% -> 5% of each run, Pallas kernels for 0% -> 0%
where the time goes in v1:
time: 368 us; the launch traced here: 367 us
  waiting for transfers between devices  226 us (61%)
  other arithmetic  62.4 us (17%)
  local copies, waits for them, and re-layouts  46.6 us (13%)
  between operations  16.6 us (5%)
  matrix products  11.9 us (3%)
    ppermute x3, waiting for transfers between devices, per_device(): lax.ppermute(ring[-1], 'col', [(dev, (dev + 1) % 4) for dev in range(4)])  193 us
    psum x1, waiting for transfers between devices, per_device(): lax.psum(jnp.where(is_root, candidate, zero_piece), 'row')  33.7 us
    convert_element_type x1, other arithmetic, per_device(): design_all = jnp.where(is_valid, all_values.astype(jnp.float32) * jnp.cos...  21.2 us
    unnamed x2, other arithmetic  19.6 us
    concatenate x1, other arithmetic, per_device(): jnp.roll(jnp.concatenate(ring[::-1], axis=1), (lax.axis_index('col') + 1)...  19.4 us
    dot_general x1, local copies, waits for them, and re-layouts, contract_rows(): lax.dot_general(left_side, right_side, (((0,), (0,)), ((), ())), preferre...  16.2 us
    unnamed x24, local copies, waits for them, and re-layouts  14.2 us
    convert_element_type x2, local copies, waits for them, and re-layouts, per_device(): all_values.astype(jnp.float32) * jnp.cos(own_angles[:, None] * orders)  12.7 us
  transfers between devices with their start and end apart: 4, of which 4 were waited for; matrix products, arithmetic and copies ran while one was open for 5% of the time, Pallas kernels for 0%

profile of v1, /device:TPU:0, one launch (start us, length us, event | category | flops | bytes accessed | tf_op | source)
XLA Modules:
  0.0 367.0 jit_solution(6194400505150147449)
XLA Ops:
  6.5 0.8 reshape.90
  7.3 0.2 multiply_reduce_fusion
  7.5 0.1 fusion.4
  7.6 0.1 fusion.8
  7.7 5.5 %copy.20 = f32[4,32,89,1,128]{4,2,1,0,3:T(8,128)} copy(bf16[4,32,89,1,128]{4,1,3,2,0:T(8,128)(2,1)} %param.8) | data formatting | bytes 8749056 | tf_op jit(solution)/shard_map/convert_element_type | solution.py:58
  13.2 7.2 %reshape.94 = f32[4,32,11392]{2,1,0:T(8,128)} reshape(f32[4,32,89,1,128]{4,2,1,0,3:T(8,128)} %copy.20) | data formatting | bytes 11665408 | tf_op jit(solution)/shard_map/convert_element_type | solution.py:58
  20.4 0.1 constant_dynamic-slice_fusion.1
  20.5 21.2 %select_convert_fusion = bf16[4,32,11392]{2,1,0:T(8,128)(2,1)S(1)} fusion(f32[4,32,11392]{2,1,0:T(8,128)} %reshape.94, f32[11392]{0:T(1024)S(1)} %fusion.4, f32[4,32]{1,0:T(4,128)S(1)} %constant_dynamic-slice_fusion.1, pred[11392]{0:T(1024)(128)(4,1)S(1)} %fusion.8), kind=kLoop, calls=%fused_computation.2 | loop fusion | flops 5832704 | bytes 8806528 | tf_op jit(solution)/shard_map/convert_element_type | solution.py:59
  41.7 3.1 collective-permute-start
  44.8 65.2 %collective-permute-done = bf16[4,32,11392]{2,1,0:T(8,128)(2,1)S(1)} collective-permute-done((bf16[4,32,11392]{2,1,0:T(8,128)(2,1)S(1)}, bf16[4,32,11392]{2,1,0:T(8,128)(2,1)S(1)}, u32[]{:S(2)}, u32[]{:S(2)}) %collective-permute-start) | collective-permute-done | bytes 2916384 | tf_op jit(solution)/shard_map/ppermute | solution.py:63
  110.1 66.2 %collective-permute-done.1 = bf16[4,32,11392]{2,1,0:T(8,128)(2,1)} collective-permute-done((bf16[4,32,11392]{2,1,0:T(8,128)(2,1)S(1)}, bf16[4,32,11392]{2,1,0:T(8,128)(2,1)}, u32[]{:S(2)}, u32[]{:S(2)}) %collective-permute-start.1) | collective-permute-done | bytes 2916384 | tf_op jit(solution)/shard_map/ppermute | solution.py:63
  177.0 0.2 select_reduce_fusion.1
  177.2 0.6 dynamic_slice.26
  179.5 0.6 dynamic_slice.27
  180.7 0.1 select_reduce_fusion
  180.8 61.1 %collective-permute-done.2 = bf16[4,32,11392]{2,1,0:T(8,128)(2,1)} collective-permute-done((bf16[4,32,11392]{2,1,0:T(8,128)(2,1)}, bf16[4,32,11392]{2,1,0:T(8,128)(2,1)}, u32[]{:S(2)}, u32[]{:S(2)}) %collective-permute-start.2) | collective-permute-done | bytes 2916384 | tf_op jit(solution)/shard_map/ppermute | solution.py:63
  241.9 2.3 constant_dynamic-update-slice_fusion.7
  244.2 2.3 constant_dynamic-update-slice_fusion.6
  246.5 0.4 constant_dynamic-update-slice_fusion.5
  247.0 19.6 %constant_dynamic-update-slice_fusion.4 = bf16[4,256,11392]{2,1,0:T(8,128)(2,1)S(1)} fusion(bf16[4,256,11392]{2,1,0:T(8,128)(2,1)S(1)} %constant_dynamic-update-slice_fusion.5, f32[4,32,11392]{2,1,0:T(8,128)S(1)} %bitcast.39, f32[11392]{0:T(1024)S(1)} %fusion.4, f32[4,32]{1,0:T(4,128)S(1)} %constant_dynamic-slice_fusion.1, pred[11392]{0:T(1024)(128)(4,1)S(1)} %fusion.8), kind=kLoop, calls=%fused_computation.22 | loop fusion | flops 5832704 | bytes 8812544
  266.6 2.2 constant_dynamic-update-slice_fusion.3
  268.8 2.2 constant_dynamic-update-slice_fusion.2
  271.0 0.4 constant_dynamic-update-slice_fusion.1
  271.4 19.4 %constant_dynamic-update-slice_fusion = bf16[4,256,11392]{2,1,0:T(8,128)(2,1)S(1)} fusion(bf16[4,256,11392]{2,1,0:T(8,128)(2,1)S(1)} %constant_dynamic-update-slice_fusion.1, f32[4,32,11392]{2,1,0:T(8,128)S(1)} %bitcast.39, f32[11392]{0:T(1024)S(1)} %fusion.4, f32[4,32]{1,0:T(4,128)S(1)} %constant_dynamic-slice_fusion.1, pred[11392]{0:T(1024)(128)(4,1)S(1)} %fusion.8), kind=kLoop, calls=%fused_computation.18 | loop fusion | flops 5832704 | bytes 8812544 | tf_op jit(solution)/shard_map/jit(_roll_dynamic)/concatenate | solution.py:64
  290.8 0.9 constant_dynamic-slice_fusion
  291.8 4.4 %copy-done.2 = bf16[4,128,11392]{2,1,0:T(8,128)(2,1)} copy-done((bf16[4,128,11392]{2,1,0:T(8,128)(2,1)}, bf16[4,128,11392]{2,1,0:T(8,128)(2,1)S(1)}, u32[]{:S(2)}) %copy-start.2) | copy-done | bytes 11665432
  296.1 0.7 dynamic-slice_select_fusion
  296.9 0.6 dynamic_slice.23
  297.5 0.8 compare_reduce_fusion
  298.3 16.2 %copy.21 = bf16[11392,512]{1,0:T(8,128)(2,1)} copy(bf16[11392,512]{0,1:T(8,128)(2,1)} %bitcast.41) | data formatting | bytes 23330816 | tf_op jit(solution)/shard_map/dot_general | solution.py:24
  314.5 33.7 %all-reduce.2.cloned.1.call-done = bf16[512,128]{1,0:T(8,128)(2,1)} async-done(((bf16[512,128]{1,0:T(8,128)(2,1)}), bf16[512,128]{1,0:T(8,128)(2,1)}) %all-reduce.2.cloned.1.call-update) | async-done | bytes 131088 | tf_op jit(solution)/shard_map/psum | solution.py:69
  348.2 11.9 %fusion = f32[89,1,1,128,128]{4,3,2,1,0:T(8,128)} fusion(f32[89,1,1,128,128]{4,3,2,1,0:T(8,128)} %param.15, pred[89]{0:T(512)(128)(4,1)S(1)} %compare_reduce_fusion, bf16[89,128,512]{2,1,0:T(8,128)(2,1)} %bitcast.37, bf16[512,128]{1,0:T(8,128)(2,1)} %all-reduce.2.cloned.1.call-done, f32[512]{0:T(512)S(1)} %multiply_multiply_fusion), kind=kOutput, calls=%fused_computation.1 | convolution fusion | flops 1496285184 | bytes 23464024 | tf_op jit(solution)/shard_map/dot_general | solution.py:24
  (25 shorter events, 0.1 us)
Async XLA Ops:
  6.5 13.9 %copy-start = (f32[512]{0:T(512)S(1)}, f32[512]{0:T(512)}, u32[]{:S(2)}) copy-start(f32[512]{0:T(512)} %param.9) | copy-start | bytes 6148
  6.5 341.6 %all-reduce.2.cloned.1.call-start = ((), (), s32[]{:S(2)}) async-start(), calls=%async_computation | async-start | bytes 262144 | tf_op jit(solution)/shard_map/psum | solution.py:69
  20.4 156.6 %copy-start.3 = (s32[712]{0:T(1024)S(1)}, s32[712]{0:T(1024)}, u32[]{:S(2)}) copy-start(s32[712]{0:T(1024)} %param.13) | copy-start | bytes 8548
  20.4 160.3 %copy-start.5 = (s32[512]{0:T(512)S(1)}, s32[512]{0:T(512)}, u32[]{:S(2)}) copy-start(s32[512]{0:T(512)} %param.12) | copy-start | bytes 6148
  20.4 160.3 %copy-start.6 = (f32[8]{0:T(128)S(1)}, f32[8]{0:T(128)}, u32[]{:S(2)}) copy-start(f32[8]{0:T(128)} %param.11) | copy-start | bytes 100
  41.7 68.3 %collective-permute-start = (bf16[4,32,11392]{2,1,0:T(8,128)(2,1)S(1)}, bf16[4,32,11392]{2,1,0:T(8,128)(2,1)S(1)}, u32[]{:S(2)}, u32[]{:S(2)}) collective-permute-start(bf16[4,32,11392]{2,1,0:T(8,128)(2,1)S(1)} %select_convert_fusion), channel_id=1, source_target_pairs={{0,1},{1,2},{2,3},{3,0},{4,5},{5,6},{6,7},{7,4},{8,9},{9,10},{10,1... | collective-permute-start | bytes 8749064 | tf_op jit(solution)/shard_map/ppermute | solution.py:63
  110.1 66.3 %collective-permute-start.1 = (bf16[4,32,11392]{2,1,0:T(8,128)(2,1)S(1)}, bf16[4,32,11392]{2,1,0:T(8,128)(2,1)}, u32[]{:S(2)}, u32[]{:S(2)}) collective-permute-start(bf16[4,32,11392]{2,1,0:T(8,128)(2,1)S(1)} %collective-permute-done), channel_id=1, source_target_pairs={{0,1},{1,2},{2,3},{3,0},{4,5},{5,6},{6,7},{7,4},{8,9},{9,10},{10,1... | collective-permute-start | bytes 8749064 | tf_op jit(solution)/shard_map/ppermute | solution.py:63
  176.3 65.6 %collective-permute-start.2 = (bf16[4,32,11392]{2,1,0:T(8,128)(2,1)}, bf16[4,32,11392]{2,1,0:T(8,128)(2,1)}, u32[]{:S(2)}, u32[]{:S(2)}) collective-permute-start(bf16[4,32,11392]{2,1,0:T(8,128)(2,1)} %collective-permute-done.1), channel_id=1, source_target_pairs={{0,1},{1,2},{2,3},{3,0},{4,5},{5,6},{6,7},{7,4},{8,9},{9,10},{10,1... | collective-permute-start | bytes 8749064 | tf_op jit(solution)/shard_map/ppermute | solution.py:63
  241.9 5.0 %slice-start = ((s8[5832704]{0:T(1024)(128)(4,1)}), s8[4194304]{0:T(1024)(128)(4,1)S(1)}, s32[]{:S(2)}) async-start(s8[5832704]{0:T(1024)(128)(4,1)} %bitcast.38), calls=%async_computation.1 | async-start | bytes 8388608
  244.2 2.7 slice-start.1
  290.8 6.0 %copy-start.4 = (f32[512]{0:T(512)S(1)}, f32[512]{0:T(512)}, u32[]{:S(2)}) copy-start(f32[512]{0:T(512)} %param.10) | copy-start | bytes 6148
  291.8 4.4 %copy-start.2 = (bf16[4,128,11392]{2,1,0:T(8,128)(2,1)}, bf16[4,128,11392]{2,1,0:T(8,128)(2,1)S(1)}, u32[]{:S(2)}) copy-start(bf16[4,128,11392]{2,1,0:T(8,128)(2,1)S(1)} %constant_dynamic-slice_fusion) | copy-start | bytes 34996228
  348.2 11.9 %copy-start.1 = (f32[512]{0:T(512)S(1)}, f32[512]{0:T(512)}, u32[]{:S(2)}) copy-start(f32[512]{0:T(512)} %param.9) | copy-start | bytes 6148
Sparse Core Ops, SparseCore 0:
  297.0 51.1 all-reduce.1
